TPU v7x, 32 devices: a whole 2x2x4 slice. The times are simulated.
32 devices in a mesh: grp: 2 (over y), tile: 16 (over z, x, core).
Axes of the slice: x: 2, y: 2, z: 4, core: 2. Of those that a mesh axis runs over, the one named last changes fastest.
Arguments:
- fields: bfloat16 [6, 128, 128, 256], P('grp', 'tile'), parts along dimension 0, may hold values from -6 to 6
- seam_tile: int32 [3, 16, 2], P(None, 'tile'), may hold values from 0 to 47, as said below
- seam_code: int32 [3, 16, 2], P(None, 'tile'), may hold values from 0 to 3
- encoder_weight: bfloat16 [3, 3, 256, 256], replicated, may hold values from -0.125 to 0.125
- encoder_bias: float32 [256], replicated, may hold values from -3 to 3
- middle_weight: bfloat16 [3, 3, 256, 256], replicated, may hold values from -0.125 to 0.125
- middle_bias: float32 [256], replicated, may hold values from -3 to 3
- upconv_weight: bfloat16 [2, 2, 256, 256], replicated, may hold values from -0.375 to 0.375
- upconv_bias: float32 [256], replicated, may hold values from -3 to 3
- decoder_weight: bfloat16 [3, 3, 512, 256], replicated, may hold values from -0.09375 to 0.09375
- decoder_offset_bias: float32 [256], replicated, may hold values from -3 to 3
Outputs:
- decoded: bfloat16 [6, 128, 128, 256], P('grp', 'tile'), parts along dimension 0
There are 2 independent parts, one for each index of `grp`. A program takes and returns all parts, laid end to end along the dimension named above; an argument that names none is the same for every part. Nothing has to cross between parts.
Inputs may be any that keep to these rules, and one draw needn't show every extreme that they name: `seam_tile`: for each side, the 12 faces (cycle, face) name 12 different partner faces; all 4 tiles of one face side share the partner face and the code, and strip s names the tile of strip s of the partner face, or of strip 4 - 1 - s where the code is 2 or more.
All inputs are finite; a program needn't handle non-finite values.
Results may differ from a plain program's by a relative error of at most 0.0048.
Values may be sent and summed in bfloat16 or wider, within the bound.
A program may use at most 128 MiB of HBM per device.

v0:
```python
import jax
import jax.numpy as jnp
from jax import lax
from jax.sharding import PartitionSpec as P


def with_halo(shard, sides, width):
    for axis, dim in sides:
        devices, length = (lax.axis_size(axis), shard.shape[dim])
        up = [(i, (i + 1) % devices) for i in range(devices)]
        down = [(j, i) for i, j in up]
        last = lax.slice_in_dim(shard, length - width, length, axis=dim)
        first = lax.slice_in_dim(shard, 0, width, axis=dim)
        before = lax.ppermute(last, axis, up)
        after = lax.ppermute(first, axis, down)
        shard = jnp.concatenate([before, shard, after], axis=dim)
    return shard


def gelu_tanh(values):
    return jax.nn.gelu(values, approximate=True)


def blank_edge_rows(extended, top_face, bottom_face):
    upper_row = extended[..., :1, :, :]
    lower_row = extended[..., -1:, :, :]
    upper_row = jnp.where(top_face, jnp.zeros_like(upper_row), upper_row)
    lower_row = jnp.where(bottom_face, jnp.zeros_like(lower_row), lower_row)
    return jnp.concatenate([upper_row, extended[..., 1:-1, :, :], lower_row], axis=-3)


def boundary_columns(extended):
    return jnp.stack([extended[..., :, 0, :], extended[..., :, -1, :]], axis=-3)


def pick_partner(flattened, partners, seam_codes):
    chosen = flattened[partners]
    column_bit = (seam_codes % 2)[..., None, None]
    single = jnp.where(column_bit == 0, chosen[..., 0, :, :], chosen[..., 1, :, :])
    mirror_flag = (seam_codes // 2)[..., None, None]
    return jnp.where(mirror_flag == 1, single[..., ::-1, :], single)


def attach_columns(extended, picked):
    left_col = picked[..., 0, :, :][..., :, None, :]
    right_col = picked[..., 1, :, :][..., :, None, :]
    return jnp.concatenate([left_col, extended, right_col], axis=-2)


def convolve(padded, weight, bias):
    leading = padded.shape[:-3]
    rows_out = padded.shape[-3] - 2
    cols_out = padded.shape[-2] - 2
    chans_in = padded.shape[-1]
    chans_out = weight.shape[-1]
    accumulated = jnp.zeros(leading + (rows_out, cols_out, chans_out), jnp.float32)
    for row_tap in range(3):
        for col_tap in range(3):
            window = padded[..., row_tap : row_tap + rows_out, col_tap : col_tap + cols_out, :]
            product = jnp.dot(
                window.reshape(-1, chans_in),
                weight[row_tap, col_tap],
                preferred_element_type=jnp.float32,
            )
            accumulated = accumulated + product.reshape(accumulated.shape)
    return accumulated + bias


def coarsen_grid(sphere_map):
    leading = sphere_map.shape[:-3]
    rows_in, cols_in, chans_in = sphere_map.shape[-3:]
    values = sphere_map.astype(jnp.float32).reshape(
        leading + (rows_in // 2, 2, cols_in // 2, 2, chans_in)
    )
    return jnp.mean(values, axis=(-4, -2)).astype(jnp.bfloat16)


def upsample(coarse, weight, bias):
    leading = coarse.shape[:-3]
    rows_in, cols_in, chans_in = coarse.shape[-3:]
    chans_out = weight.shape[-1]
    flattened = coarse.reshape(-1, chans_in)
    phases = []
    for row_phase in range(2):
        phase_row = []
        for col_phase in range(2):
            product = jnp.dot(
                flattened, weight[row_phase, col_phase], preferred_element_type=jnp.float32
            )
            phase_row.append(product.reshape(leading + (rows_in, cols_in, chans_out)))
        phases.append(
            jnp.stack(phase_row, axis=-2).reshape(leading + (rows_in, 2 * cols_in, chans_out))
        )
    full = jnp.stack(phases, axis=-3).reshape(leading + (2 * rows_in, 2 * cols_in, chans_out))
    return (full + bias).astype(jnp.bfloat16)


def flatten_gathered(gathered):
    return gathered.reshape((-1,) + gathered.shape[2:])


def on_device(
    fields,
    seam_tile,
    seam_code,
    encoder_weight,
    encoder_bias,
    middle_weight,
    middle_bias,
    upconv_weight,
    upconv_bias,
    decoder_weight,
    decoder_offset_bias,
):
    strip_count = lax.axis_size("tile") // 4
    strip_index = (lax.axis_index("tile") + strip_count // 2) % strip_count
    top_face = strip_index == 0
    bottom_face = strip_index == strip_count - 1
    partners = seam_tile[:, 0, :]
    seam_codes = seam_code[:, 0, :]
    extended = blank_edge_rows(with_halo(fields, (("tile", 1),), 1), top_face, bottom_face)
    gathered = lax.all_gather(boundary_columns(extended)[:, None], "tile", axis=1, tiled=True)
    padded = attach_columns(
        extended, pick_partner(flatten_gathered(gathered), partners, seam_codes)
    )
    shortcut_map = gelu_tanh(convolve(padded, encoder_weight, encoder_bias)).astype(jnp.bfloat16)
    averaged_map = coarsen_grid(shortcut_map)
    extended = blank_edge_rows(with_halo(averaged_map, (("tile", 1),), 1), top_face, bottom_face)
    gathered = lax.all_gather(boundary_columns(extended)[:, None], "tile", axis=1, tiled=True)
    padded = attach_columns(
        extended, pick_partner(flatten_gathered(gathered), partners, seam_codes)
    )
    coarse = gelu_tanh(convolve(padded, middle_weight, middle_bias)).astype(jnp.bfloat16)
    upsampled = upsample(coarse, upconv_weight, upconv_bias)
    joined = jnp.concatenate([upsampled, shortcut_map], axis=-1)
    joined_ext = blank_edge_rows(with_halo(joined, (("tile", 1),), 1), top_face, bottom_face)
    gathered = lax.all_gather(boundary_columns(joined_ext)[:, None], "tile", axis=1, tiled=True)
    padded = attach_columns(
        joined_ext, pick_partner(flatten_gathered(gathered), partners, seam_codes)
    )
    return convolve(padded, decoder_weight, decoder_offset_bias).astype(jnp.bfloat16)


def solution(mesh):
    return jax.shard_map(
        on_device,
        mesh=mesh,
        in_specs=(
            P("grp", "tile", None, None),
            P(None, "tile", None),
            P(None, "tile", None),
            P(),
            P(),
            P(),
            P(),
            P(),
            P(),
            P(),
            P(),
        ),
        out_specs=P("grp", "tile", None, None),
        check_vma=False,
    )
```

profile of v0, /device:TPU:0, one launch (start us, length us, event | category | flops | bytes accessed | tf_op | source)
XLA Modules:
  0.0 164.7 jit_solution(4642079154385857864)
XLA Ops:
  0.0 1.0 fusion.168
  1.1 0.5 collective-permute-start
  1.6 5.0 %collective-permute-start.1 = (bf16[3,1,128,256]{3,2,1,0:T(8,128)(2,1)S(1)}, bf16[3,1,128,256]{3,2,1,0:T(8,128)(2,1)S(1)}, u32[]{:S(2)}, u32[]{:S(2)}) collective-permute-start(bf16[3,1,128,256]{3,2,1,0:T(8,128)(2,1)S(1)} %get-tuple-element.16), channel_id=1, source_target_pairs={{1,0},{2,1},{3,2},{4,3},{5,4},{6,5},{7,6},{8,7},{9,8},{10,9},{11,1... | collective-permute-start | bytes 589832 | tf_op jit(solution)/shard_map/ppermute | solution.py:15
  6.6 0.7 compare_select_fusion
  7.3 3.8 %fusion.131 = f32[3,8,128,256]{3,2,1,0:T(8,128)} fusion(bf16[3,8,128,256]{3,2,1,0:T(8,128)(2,1)} %param.11, bf16[3,3,256,256]{3,2,1,0:T(8,128)(2,1)} %param.14), kind=kOutput, calls=%fused_computation.154 | convolution fusion | flops 402653184 | bytes 4849664 | tf_op jit(solution)/shard_map/dot_general | solution.py:60
  11.6 3.1 %fusion.40 = f32[3,8,128,256]{3,2,1,0:T(8,128)} fusion(bf16[3,1,128,256]{3,2,1,0:T(8,128)(2,1)S(1)} %broadcast_select_fusion.2, bf16[3,8,128,256]{3,2,1,0:T(8,128)(2,1)S(1)} %copy-done, bf16[3,3,256,256]{3,2,1,0:T(8,128)(2,1)} %param.14), kind=kOutput, calls=%fused_computation.51 | convolution fusion | flops 406192128 | bytes 5046272 | tf_op jit(solution)/shard_map/dot_general | solution.py:60
  14.8 3.2 %fusion.36 = f32[3,8,128,256]{3,2,1,0:T(8,128)} fusion(bf16[3,8,128,256]{3,2,1,0:T(8,128)(2,1)S(1)} %copy-done, bf16[3,1,128,256]{3,2,1,0:T(8,128)(2,1)S(1)} %broadcast_select_fusion.3, bf16[3,3,256,256]{3,2,1,0:T(8,128)(2,1)} %param.14), kind=kOutput, calls=%fused_computation.47 | convolution fusion | flops 406192128 | bytes 5046272 | tf_op jit(solution)/shard_map/dot_general | solution.py:60
  18.0 21.6 %all-gather = bf16[3,32,10,256]{3,0,2,1:T(4,128)(2,1)S(1)} all-gather(bf16[3,2,10,256]{3,0,2,1:T(4,128)(2,1)S(1)} %pad_maximum_fusion.13), channel_id=2, replica_groups=mesh['grp'=2,'tile'=16] {'tile'}, dimensions={1}, use_global_device_ids=true | all-gather | bytes 522240 | tf_op jit(solution)/shard_map/all_gather | solution.py:122
  39.7 0.2 reshape.236
  39.9 0.7 gather_fusion
  41.1 1.1 pad_maximum_fusion.2
  42.3 0.6 fusion.50
  42.9 0.6 fusion.54
  43.5 0.6 fusion.48
  44.0 0.6 fusion.52
  44.6 0.6 fusion.56
  45.2 1.3 copy-done.1
  46.5 4.6 %fusion.19 = bf16[3,8,128,256]{3,2,1,0:T(8,128)(2,1)S(1)} fusion(f32[3,8,128,256]{3,2,1,0:T(8,128)} %fusion.40, f32[3,8,128,256]{3,2,1,0:T(8,128)S(1)} %fusion.48, f32[3,8,128,256]{3,2,1,0:T(8,128)S(1)} %fusion.50, f32[3,8,128,256]{3,2,1,0:T(8,128)S(1)} %copy-done.1, f32[3,8,128,256]{3,2,1,0:T(8,128)S(1)} %fusion.52, f32[3,8,128,256]{3,2,1,0:T(8,128)S(1)} %fusion.54, ...), kind=kOutput, calls=%fused_computation.25 | convolution fusion | flops 416808960 | bytes 28443648 | tf_op jit(solution)/shard_map/dot_general | solution.py:60
  51.1 3.0 %reshape.243 = f32[3,4,2,64,2,256]{5,4,3,2,1,0:T(2,128)} reshape(bf16[3,8,128,256]{3,2,1,0:T(8,128)(2,1)S(1)} %fusion.19) | data formatting | bytes 4718592 | tf_op jit(solution)/shard_map/reshape | solution.py:72
  54.1 4.3 %reduce_sum.9 = f32[3,4,64,256]{3,2,1,0:T(8,128)S(1)} reduce(f32[3,4,2,64,2,256]{5,4,3,2,1,0:T(2,128)} %reshape.243, f32[]{:T(128)} %constant.78.clone.1), dimensions={2,4}, to_apply=%region_0.1 | reduce | flops 589824 | bytes 3932164 | tf_op jit(solution)/shard_map/reduce_sum | solution.py:75
  58.5 0.4 collective-permute-start.2
  58.9 4.1 %collective-permute-start.3 = (bf16[3,1,64,256]{3,2,1,0:T(8,128)(2,1)S(1)}, bf16[3,1,64,256]{3,2,1,0:T(8,128)(2,1)S(1)}, u32[]{:S(2)}, u32[]{:S(2)}) collective-permute-start(bf16[3,1,64,256]{3,2,1,0:T(8,128)(2,1)S(1)} %get-tuple-element.22), channel_id=1, source_target_pairs={{1,0},{2,1},{3,2},{4,3},{5,4},{6,5},{7,6},{8,7},{9,8},{10,9},{11,1... | collective-permute-start | bytes 294920 | tf_op jit(solution)/shard_map/ppermute | solution.py:15
  63.0 1.2 fusion.121
  64.2 1.1 collective-permute-done.2
  65.4 19.2 %all-gather.1 = bf16[3,32,6,256]{3,2,0,1:T(8,128)(2,1)S(1)} all-gather(bf16[3,2,6,256]{3,2,0,1:T(8,128)(2,1)S(1)} %pad_maximum_fusion.17), channel_id=3, replica_groups=mesh['grp'=2,'tile'=16] {'tile'}, dimensions={1}, use_global_device_ids=true | all-gather | bytes 313344 | tf_op jit(solution)/shard_map/all_gather | solution.py:129
  84.9 0.6 gather_fusion.1
  85.8 0.4 maximum_maximum_fusion.2
  86.2 1.2 fusion.81
  87.4 0.3 fusion.85
  87.7 0.3 fusion.89
  87.9 0.3 fusion.79
  88.2 0.3 fusion.83
  88.5 0.3 fusion.87
  88.8 0.4 fusion.64
  89.2 0.2 copy-done.11
  89.4 0.5 fusion.72
  89.9 0.5 copy-done.5
  90.5 0.3 convolution_bitcast_fusion
  90.7 0.3 convolution_bitcast_fusion.1
  91.0 0.3 convolution_bitcast_fusion.2
  91.3 0.3 convolution_bitcast_fusion.3
  91.7 1.0 copy.159
  92.8 1.0 copy.158
  93.9 0.7 pad_maximum_fusion.1
  94.6 0.5 copy.160
  95.3 0.4 add_convert_fusion.1
  95.7 1.4 collective-permute-start.5
  97.2 3.6 %fusion.32 = f32[3,8,128,256]{3,2,1,0:T(8,128)} fusion(bf16[3,8,128,256]{3,2,1,0:T(8,128)(2,1)S(1)} %fusion.19, bf16[3,8,128,256]{3,2,1,0:T(8,128)(2,1)S(1)} %add_convert_fusion.1, bf16[3,3,512,256]{3,2,1,0:T(8,128)(2,1)} %param.20), kind=kOutput, calls=%fused_computation.39 | convolution fusion | flops 811597824 | bytes 6553600 | tf_op jit(solution)/shard_map/dot_general | solution.py:60
  100.8 1.7 %collective-permute-done.5 = bf16[3,1,128,512]{3,2,1,0:T(8,128)(2,1)S(1)} collective-permute-done((bf16[3,1,128,512]{3,2,1,0:T(8,128)(2,1)S(1)}, bf16[3,1,128,512]{3,2,1,0:T(8,128)(2,1)S(1)}, u32[]{:S(2)}, u32[]{:S(2)}) %collective-permute-start.5) | collective-permute-done | bytes 393248 | tf_op jit(solution)/shard_map/ppermute | solution.py:15
  102.5 3.6 %fusion.6 = f32[3,8,128,256]{3,2,1,0:T(8,128)} fusion(bf16[3,1,128,512]{3,2,1,0:T(8,128)(2,1)S(1)} %broadcast_select_fusion, bf16[3,8,128,256]{3,2,1,0:T(8,128)(2,1)S(1)} %fusion.19, bf16[3,8,128,256]{3,2,1,0:T(8,128)(2,1)S(1)} %add_convert_fusion.1, bf16[3,3,512,256]{3,2,1,0:T(8,128)(2,1)} %param.20), kind=kOutput, calls=%fused_computation.12 | convolution fusion | flops 815923200 | bytes 6946816 | tf_op jit(solution)/shard_map/dot_general | solution.py:60
  106.1 1.1 collective-permute-done.4
  107.3 3.7 %fusion = f32[3,8,128,256]{3,2,1,0:T(8,128)} fusion(bf16[3,8,128,256]{3,2,1,0:T(8,128)(2,1)S(1)} %fusion.19, bf16[3,8,128,256]{3,2,1,0:T(8,128)(2,1)S(1)} %add_convert_fusion.1, bf16[3,1,128,512]{3,2,1,0:T(8,128)(2,1)S(1)} %broadcast_select_fusion.1, bf16[3,3,512,256]{3,2,1,0:T(8,128)(2,1)} %param.20), kind=kOutput, calls=%fused_computation.6 | convolution fusion | flops 815923200 | bytes 6946816 | tf_op jit(solution)/shard_map/dot_general | solution.py:60
  111.1 25.0 %all-gather.2 = bf16[3,32,10,512]{3,0,2,1:T(4,128)(2,1)S(1)} all-gather(bf16[3,2,10,512]{3,0,2,1:T(4,128)(2,1)S(1)} %pad_maximum_fusion.8), channel_id=4, replica_groups=mesh['grp'=2,'tile'=16] {'tile'}, dimensions={1}, use_global_device_ids=true | all-gather | bytes 1044480 | tf_op jit(solution)/shard_map/all_gather | solution.py:137
  136.1 1.3 copy.163
  137.4 3.2 %reshape.241 = bf16[48,2,10,512]{3,1,0,2:T(2,128)(2,1)} reshape(bf16[3,32,10,512]{3,1,0,2:T(8,128)(2,1)} %copy.163) | data formatting | bytes 1966080 | tf_op jit(solution)/shard_map/reshape | solution.py:99
  140.6 2.7 %gather_fusion.2 = bf16[6,2,10,512]{3,1,2,0:T(2,128)(2,1)} fusion(bf16[48,2,10,512]{3,1,0,2:T(2,128)(2,1)} %reshape.241, s32[1024]{0:T(1024)S(1)} %pad_clamp_fusion), kind=kCustom, calls=%fused_computation.2 | custom fusion | bytes 245784 | tf_op jit(solution)/shard_map/gather | solution.py:37
  143.3 1.2 fusion.170
  145.1 3.4 %pad_maximum_fusion = (bf16[3,10,129,512]{3,2,1,0:T(8,128)(2,1)S(1)}, bf16[3,10,129,512]{3,2,1,0:T(8,128)(2,1)S(1)}) fusion(bf16[3,10,1,512]{3,2,1,0:T(2,128)(2,1)S(1)} %copy.169, bf16[3,1,128,512]{3,2,1,0:T(8,128)(2,1)S(1)} %broadcast_select_fusion, bf16[3,8,128,256]{3,2,1,0:T(8,128)(2,1)S(1)} %fusion.19, bf16[3,8,128,256]{3,2,1,0:T(8,128)(2,1)S(1)} %add_convert_fusion.1, ...), kind=kLoop, calls=%fused_computation.5 | loop fusion | flops 39628800 | bytes 11919360 | tf_op jit(solution)/shard_map/concatenate | solution.py:47
  148.5 2.7 %fusion.24 = f32[3,8,128,256]{3,2,1,0:T(8,128)} fusion(bf16[3,10,129,512]{3,2,1,0:T(8,128)(2,1)S(1)} %get-tuple-element.5, bf16[3,3,512,256]{3,2,1,0:T(8,128)(2,1)S(1)} %copy-done.6), kind=kOutput, calls=%fused_computation.30 | convolution fusion | flops 805306368 | bytes 6553600 | tf_op jit(solution)/shard_map/dot_general | solution.py:60
  151.2 2.6 %fusion.28 = f32[3,8,128,256]{3,2,1,0:T(8,128)} fusion(bf16[3,10,129,512]{3,2,1,0:T(8,128)(2,1)S(1)} %get-tuple-element.5, bf16[3,3,512,256]{3,2,1,0:T(8,128)(2,1)S(1)} %copy-done.6), kind=kOutput, calls=%fused_computation.34 | convolution fusion | flops 805306368 | bytes 6553600 | tf_op jit(solution)/shard_map/dot_general | solution.py:60
  153.8 1.0 fusion.22
  154.8 1.0 fusion.26
  155.8 1.0 fusion.30
  156.8 7.9 %add_convert_fusion = bf16[3,8,128,256]{3,2,1,0:T(8,128)(2,1)} fusion(f32[3,8,128,256]{3,2,1,0:T(8,128)} %fusion.6, f32[3,8,128,256]{3,2,1,0:T(8,128)S(1)} %fusion.22, f32[3,8,128,256]{3,2,1,0:T(8,128)} %fusion.24, f32[3,8,128,256]{3,2,1,0:T(8,128)} %fusion.32, f32[3,8,128,256]{3,2,1,0:T(8,128)S(1)} %fusion.26, f32[3,8,128,256]{3,2,1,0:T(8,128)} %fusion.28, ...), kind=kOutput, calls=%fused_computation.43 | convolution fusion | flops 813170688 | bytes 30147584 | tf_op jit(solution)/shard_map/dot_general | solution.py:60
  (75 shorter events, 3.0 us)
Async XLA Ops:
  1.1 13.6 %collective-permute-start = (bf16[3,1,128,256]{3,2,1,0:T(8,128)(2,1)S(1)}, bf16[3,1,128,256]{3,2,1,0:T(8,128)(2,1)S(1)}, u32[]{:S(2)}, u32[]{:S(2)}) collective-permute-start(bf16[3,1,128,256]{3,2,1,0:T(8,128)(2,1)S(1)} %get-tuple-element.15), channel_id=1, source_target_pairs={{0,1},{1,2},{2,3},{3,4},{4,5},{5,6},{6,7},{7,8},{8,9},{9,10},{10,1... | collective-permute-start | bytes 589832 | tf_op jit(solution)/shard_map/ppermute | solution.py:14
  1.6 9.9 %collective-permute-start.1 = (bf16[3,1,128,256]{3,2,1,0:T(8,128)(2,1)S(1)}, bf16[3,1,128,256]{3,2,1,0:T(8,128)(2,1)S(1)}, u32[]{:S(2)}, u32[]{:S(2)}) collective-permute-start(bf16[3,1,128,256]{3,2,1,0:T(8,128)(2,1)S(1)} %get-tuple-element.16), channel_id=1, source_target_pairs={{1,0},{2,1},{3,2},{4,3},{5,4},{6,5},{7,6},{8,7},{9,8},{10,9},{11,1... | collective-permute-start | bytes 589832 | tf_op jit(solution)/shard_map/ppermute | solution.py:15
  7.3 3.8 %copy-start.10 = (s32[3,1,2]{0,2,1:T(2,128)S(1)}, s32[3,1,2]{0,2,1:T(2,128)}, u32[]{:S(2)}) copy-start(s32[3,1,2]{0,2,1:T(2,128)} %param.13) | copy-start | bytes 76
  7.3 4.3 %copy-start = (bf16[3,8,128,256]{3,2,1,0:T(8,128)(2,1)S(1)}, bf16[3,8,128,256]{3,2,1,0:T(8,128)(2,1)}, u32[]{:S(2)}) copy-start(bf16[3,8,128,256]{3,2,1,0:T(8,128)(2,1)} %param.11) | copy-start | bytes 4718596
  41.0 1.3 copy-start.3
  44.6 1.9 %copy-start.1 = (f32[3,8,128,256]{3,2,1,0:T(8,128)S(1)}, f32[3,8,128,256]{3,2,1,0:T(8,128)}, u32[]{:S(2)}) copy-start(f32[3,8,128,256]{3,2,1,0:T(8,128)} %fusion.131) | copy-start | bytes 9437188
  44.6 1.9 %copy-start.8 = (f32[256]{0:T(256)S(1)}, f32[256]{0:T(256)}, u32[]{:S(2)}) copy-start(f32[256]{0:T(256)} %param.15) | copy-start | bytes 3076
  58.5 6.8 %collective-permute-start.2 = (bf16[3,1,64,256]{3,2,1,0:T(8,128)(2,1)S(1)}, bf16[3,1,64,256]{3,2,1,0:T(8,128)(2,1)S(1)}, u32[]{:S(2)}, u32[]{:S(2)}) collective-permute-start(bf16[3,1,64,256]{3,2,1,0:T(8,128)(2,1)S(1)} %get-tuple-element.21), channel_id=1, source_target_pairs={{0,1},{1,2},{2,3},{3,4},{4,5},{5,6},{6,7},{7,8},{8,9},{9,10},{10,1... | collective-permute-start | bytes 294920 | tf_op jit(solution)/shard_map/ppermute | solution.py:14
  58.9 6.4 %collective-permute-start.3 = (bf16[3,1,64,256]{3,2,1,0:T(8,128)(2,1)S(1)}, bf16[3,1,64,256]{3,2,1,0:T(8,128)(2,1)S(1)}, u32[]{:S(2)}, u32[]{:S(2)}) collective-permute-start(bf16[3,1,64,256]{3,2,1,0:T(8,128)(2,1)S(1)} %get-tuple-element.22), channel_id=1, source_target_pairs={{1,0},{2,1},{3,2},{4,3},{5,4},{6,5},{7,6},{8,7},{9,8},{10,9},{11,1... | collective-permute-start | bytes 294920 | tf_op jit(solution)/shard_map/ppermute | solution.py:15
  85.5 1.9 %copy-start.4 = (bf16[3,3,256,256]{3,2,1,0:T(8,128)(2,1)S(1)}, bf16[3,3,256,256]{3,2,1,0:T(8,128)(2,1)}, u32[]{:S(2)}) copy-start(bf16[3,3,256,256]{3,2,1,0:T(8,128)(2,1)} %param.16) | copy-start | bytes 3538948
  88.8 0.7 copy-start.11
  89.4 1.0 copy-start.5
  94.6 0.7 copy-start.9
  95.7 6.7 %collective-permute-start.5 = (bf16[3,1,128,512]{3,2,1,0:T(8,128)(2,1)S(1)}, bf16[3,1,128,512]{3,2,1,0:T(8,128)(2,1)S(1)}, u32[]{:S(2)}, u32[]{:S(2)}) collective-permute-start(bf16[3,1,128,512]{3,2,1,0:T(8,128)(2,1)S(1)} %get-tuple-element.10), channel_id=1, source_target_pairs={{1,0},{2,1},{3,2},{4,3},{5,4},{6,5},{7,6},{8,7},{9,8},{10,9},{11,1... | collective-permute-start | bytes 1179656 | tf_op jit(solution)/shard_map/ppermute | solution.py:15
  97.2 10.0 %collective-permute-start.4 = (bf16[3,1,128,512]{3,2,1,0:T(8,128)(2,1)S(1)}, bf16[3,1,128,512]{3,2,1,0:T(8,128)(2,1)S(1)}, u32[]{:S(2)}, u32[]{:S(2)}) collective-permute-start(bf16[3,1,128,512]{3,2,1,0:T(8,128)(2,1)S(1)} %get-tuple-element.9), channel_id=1, source_target_pairs={{0,1},{1,2},{2,3},{3,4},{4,5},{5,6},{6,7},{7,8},{8,9},{9,10},{10,1... | collective-permute-start | bytes 1179656 | tf_op jit(solution)/shard_map/ppermute | solution.py:14
  107.2 3.8 %copy-start.2 = (bf16[3,1,128,512]{3,2,1,0:T(8,128)(2,1)}, bf16[3,1,128,512]{3,2,1,0:T(8,128)(2,1)S(1)}, u32[]{:S(2)}) copy-start(bf16[3,1,128,512]{3,2,1,0:T(8,128)(2,1)S(1)} %broadcast_select_fusion.1) | copy-start | bytes 1179652
  145.0 3.4 %copy-start.6 = (bf16[3,3,512,256]{3,2,1,0:T(8,128)(2,1)S(1)}, bf16[3,3,512,256]{3,2,1,0:T(8,128)(2,1)}, u32[]{:S(2)}) copy-start(bf16[3,3,512,256]{3,2,1,0:T(8,128)(2,1)} %param.20) | copy-start | bytes 7077892
  155.8 1.0 copy-start.7
where the time goes:
time: 165 us
  blocking collectives  65.8 us (40%)
  matrix products  50.2 us (30%)
  local copies, waits for them, and re-layouts  20.2 us (12%)
  other arithmetic  12.4 us (8%)
  starting transfers between devices  11.5 us (7%)
  waiting for transfers between devices  3.92 us (2%)
    dot_general x27, matrix products, convolve(): jnp.dot(window.reshape(-1, chans_in), weight[row_tap, col_tap], preferred...  49.1 us
    all_gather x2, blocking collectives, on_device(): lax.all_gather(boundary_columns(extended)[:, None], 'tile', axis=1, tiled...  40.8 us
    all_gather x1, blocking collectives, on_device(): lax.all_gather(boundary_columns(joined_ext)[:, None], 'tile', axis=1, til...  25 us
    ppermute x3, starting transfers between devices, with_halo(): after = lax.ppermute(first, axis, down)  10.5 us
    concatenate x3, other arithmetic, attach_columns(): return jnp.concatenate([left_col, extended, right_col], axis=-2)  4.9 us
    reduce_sum x1, other arithmetic, coarsen_grid(): return jnp.mean(values, axis=(-4, -2)).astype(jnp.bfloat16)  4.28 us
    gather x3, local copies, waits for them, and re-layouts, pick_partner(): chosen = flattened[partners]  4.01 us
    reshape x3, local copies, waits for them, and re-layouts, flatten_gathered(): return gathered.reshape((-1,) + gathered.shape[2:])  3.5 us
  transfers between devices with their start and end apart: 6, of which 3 were waited for; matrix products, arithmetic and copies ran while one was open for 10% of the time, Pallas kernels for 0%

commit v1 on v0

v1 whole, which is shorter than its diff:
```python
import functools

import jax
import jax.numpy as jnp
from jax import lax
from jax.experimental import pallas as pl
from jax.experimental.pallas import tpu as pltpu
from jax.sharding import PartitionSpec as P

F32 = jnp.float32
BF16 = jnp.bfloat16
FACES = 4


def gelu_tanh(x):
    return 0.5 * x * (1.0 + jnp.tanh(0.7978845608 * (x + 0.044715 * (x * x * x))))


def kernel(
    tiles,
    seam_tile,
    seam_code,
    fields_hbm,
    enc_w_hbm,
    mid_w_hbm,
    up_w_hbm,
    dec_w_hbm,
    enc_b,
    mid_b,
    up_b,
    dec_b,
    out,
    fields,
    enc_w,
    mid_w,
    up_w,
    dec_w,
    x_enc,
    x_skip,
    x_pool,
    x_up,
    acc_enc,
    acc_dec,
    coarse,
    fine,
    pair,
    corner_tmp,
    edge_tmp,
    seam_tmp,
    corner_src,
    corner_dst,
    halo,
    halo_pool,
    edges,
    edges_pool,
    recv_enc,
    recv_skip,
    recv_up,
    recv_pool,
    load_sem,
    send_sem,
    recv_sem,
):
    cycles, h, cols, ch = fields.shape
    hc, cc = h // 2, cols // 2
    strips = tiles // FACES
    me = lax.axis_index("tile")
    place = lax.rem(me + strips // 2, tiles)
    face = place // strips
    strip = place - face * strips
    top_face = strip == 0
    bottom_face = strip == strips - 1
    up_tile = lax.rem(me + tiles - 1, tiles)
    down_tile = lax.rem(me + 1, tiles)

    def tile_of(f, s):
        return lax.rem(f * strips + s + tiles - strips // 2, tiles)

    peers = []
    for kind in range(2):
        s = strip if kind == 0 else strips - 1 - strip
        for j in range(1 - kind, FACES):
            f = lax.rem(face + j, FACES)
            peers.append((kind, f, tile_of(f, s)))

    loads = []
    for k, (src, dst) in enumerate(
        ((fields_hbm, fields), (enc_w_hbm, enc_w), (dec_w_hbm, dec_w), (mid_w_hbm, mid_w), (up_w_hbm, up_w))
    ):
        copy = pltpu.make_async_copy(src, dst, load_sem.at[k])
        copy.start()
        loads.append(copy)

    barrier = pltpu.get_barrier_semaphore()
    targets = [up_tile, down_tile] + [peer for _, _, peer in peers]
    for target in targets:
        pl.semaphore_signal(barrier, inc=1, device_id={"tile": target})
    pl.semaphore_wait(barrier, len(targets))

    def remote(src, dst, e, send_at, recv_at, target):
        return pltpu.make_async_remote_copy(
            src_ref=src,
            dst_ref=dst,
            send_sem=send_sem.at[e, send_at],
            recv_sem=recv_sem.at[e, recv_at],
            device_id={"tile": target},
        )

    def spread(x, i, r, value):
        width = value.shape[0]
        at = lax.broadcasted_iota(jnp.int32, value.shape, 0)
        left = jnp.where(at == 0, 0.0, pltpu.roll(value, 1, 0))
        right = jnp.where(at == width - 1, 0.0, pltpu.roll(value, width - 1, 0))
        x[i, r, :, 0:ch] = left.astype(BF16)
        x[i, r, :, ch : 2 * ch] = value.astype(BF16)
        x[i, r, :, 2 * ch : 3 * ch] = right.astype(BF16)

    class Exchange:
        def __init__(self, e, x, halo_ref, edge_ref, recv_ref):
            self.e, self.x, self.halo, self.edges, self.recv = e, x, halo_ref, edge_ref, recv_ref
            self.rows = x.shape[0] - 2
            self.width = x.shape[2]

        def end_pixels(self, i, r):
            head = self.x[i, r, 0:16, ch : 2 * ch].astype(F32)[0:1]
            tail = self.x[i, r, self.width - 16 : self.width, ch : 2 * ch].astype(F32)[15:16]
            return head, tail

        def send_rows(self):
            e, x, rows = self.e, self.x, self.rows
            for which, i in ((0, 1), (1, rows)):
                for r in range(cycles):
                    head, tail = self.end_pixels(i, r)
                    corner_tmp[e, which, 2 * r : 2 * r + 1, :] = head
                    corner_tmp[e, which, 2 * r + 1 : 2 * r + 2, :] = tail
                corner_src[e, which] = corner_tmp[e, which].astype(BF16)
            self.copies = [
                remote(corner_src.at[e, 1], corner_dst.at[e, 0], e, 0, 0, down_tile),
                remote(corner_src.at[e, 0], corner_dst.at[e, 1], e, 1, 1, up_tile),
                remote(x.at[rows, :, :, ch : 2 * ch], self.halo.at[0], e, 2, 2, down_tile),
                remote(x.at[1, :, :, ch : 2 * ch], self.halo.at[1], e, 3, 3, up_tile),
            ]
            for copy in self.copies:
                copy.start()

        def send_edges(self):
            e, rows = self.e, self.rows
            self.copies[0].wait_recv()
            self.copies[1].wait_recv()
            above = jnp.where(top_face, 0.0, corner_dst[e, 0].astype(F32))
            below = jnp.where(bottom_face, 0.0, corner_dst[e, 1].astype(F32))
            for r in range(cycles):
                for side in range(2):
                    k = 2 * r + side
                    edge_tmp[e, k, 0:1, :] = above[k : k + 1]
                    edge_tmp[e, k, rows + 1 : rows + 2, :] = below[k : k + 1]
                for i in range(rows):
                    for side, pixel in enumerate(self.end_pixels(i + 1, r)):
                        edge_tmp[e, 2 * r + side, i + 1 : i + 2, :] = pixel
            value = edge_tmp[e, :, 0 : rows + 2, :].astype(BF16)
            self.edges[...] = value
            self.recv[face] = value
            self.seams = [
                remote(
                    self.edges,
                    self.recv.at[kind * FACES + face],
                    e,
                    4 + kind * FACES + f,
                    4 + kind * FACES + face,
                    peer,
                )
                for kind, f, peer in peers
            ]
            for copy in self.seams:
                copy.start()

        def wait_rows(self):
            self.copies[2].wait_recv()
            self.copies[3].wait_recv()
            for r in range(cycles):
                above = jnp.where(top_face, 0.0, self.halo[0, r].astype(F32))
                spread(self.x, 0, r, above)
                below = jnp.where(bottom_face, 0.0, self.halo[1, r].astype(F32))
                spread(self.x, self.rows + 1, r, below)

        def seam_terms(self, weight_of):
            e, rows = self.e, self.rows
            for kind, f, peer in peers:
                slot = kind * FACES + f
                remote(self.edges, self.recv.at[slot], e, 4 + slot, 4 + slot, peer).wait_recv()
            for copy in self.copies + self.seams:
                copy.wait_send()
            terms = []
            for side in range(2):
                for r in range(cycles):
                    partner, code = seam_tile[r, side], seam_code[r, side]
                    cycle = partner // tiles
                    home = lax.rem(partner - cycle * tiles + strips // 2, tiles) // strips
                    mirrored = code >= 2
                    slot = jnp.where(mirrored, FACES, 0) + home
                    column = self.recv[slot, 2 * cycle + lax.rem(code, 2)].astype(F32)
                    for i in range(rows + 2):
                        seam_tmp[side, r, i : i + 1, :] = jnp.where(
                            mirrored, column[rows + 1 - i : rows + 2 - i], column[i : i + 1]
                        )
                taps = [
                    jnp.concatenate([seam_tmp[side, r, a : a + 8, :] for r in range(cycles)], axis=0).astype(BF16)
                    for a in range(3)
                ]
                term = jnp.zeros((8 * cycles, ch), F32)
                for a in range(3):
                    term = term + jnp.dot(taps[a], weight_of(a, 2 * side), preferred_element_type=F32)
                terms.append(term)
            return terms

        def add_seams(self, acc, weight_of):
            terms = self.seam_terms(weight_of)
            for side in range(2):
                j = 0 if side == 0 else self.width - 1
                for r in range(cycles):
                    for i in range(self.rows):
                        acc[i, r, j : j + 1, :] += terms[side][8 * r + i : 8 * r + i + 1]

    def conv_rows(x, start, count, weights):
        width = x.shape[2]
        taps = [x[pl.ds(start + a, count)].reshape(count * cycles * width, 3 * ch) for a in range(3)]
        product = jnp.dot(jnp.concatenate(taps, axis=1), weights(), preferred_element_type=F32)
        return product.reshape(count, cycles, width, ch)

    def enc_weights():
        return enc_w[...].reshape(9 * ch, ch)

    def mid_weights():
        return mid_w[...].reshape(9 * ch, ch)

    def dec_weights(part):
        def get():
            picked = [dec_w[a, b, part * ch : (part + 1) * ch, :] for a in range(3) for b in range(3)]
            return jnp.concatenate(picked, axis=0)

        return get

    def dec_tap(part):
        return lambda a, b: dec_w[a, b, part * ch : (part + 1) * ch, :]

    loads[0].wait()

    @pl.loop(0, h)
    def _(i):
        for r in range(cycles):
            spread(x_enc, i + 1, r, fields[r, i].astype(F32))

    enc = Exchange(0, x_enc, halo.at[0], edges.at[0], recv_enc)
    enc.send_rows()
    loads[1].wait()

    def inner_rows(x, acc, weights, lo, hi, add):
        @pl.loop(lo, hi)
        def _(k):
            start = 1 + 2 * k
            value = conv_rows(x, start, 2, weights)
            if add:
                acc[pl.ds(start, 2)] += value
            else:
                acc[pl.ds(start, 2)] = value

    inner = (h - 2) // 2
    inner_rows(x_enc, acc_enc, enc_weights, 0, 1, False)
    enc.send_edges()
    inner_rows(x_enc, acc_enc, enc_weights, 1, inner, False)
    enc.wait_rows()

    def outer_rows(x, acc, weights, add):
        @pl.loop(0, 2)
        def _(k):
            i = k * (h - 1)
            value = conv_rows(x, i, 1, weights)
            if add:
                acc[pl.ds(i, 1)] += value
            else:
                acc[pl.ds(i, 1)] = value

    outer_rows(x_enc, acc_enc, enc_weights, False)
    enc.add_seams(acc_enc, lambda a, b: enc_w[a, b])

    @pl.loop(0, hc)
    def _(q):
        for r in range(cycles):
            total = None
            for a in range(2):
                value = gelu_tanh(acc_enc[2 * q + a, r] + enc_b[...]).astype(BF16).astype(F32)
                spread(x_skip, 2 * q + a + 1, r, value)
                total = value if total is None else total + value
            halves = []
            for k in range(ch // 128):
                pair[r, k] = total[:, k * 128 : (k + 1) * 128]
                even = pair[r, k, pl.ds(0, cc, stride=2), :]
                odd = pair[r, k, pl.ds(1, cc, stride=2), :]
                halves.append((even + odd) * 0.25)
            spread(x_pool, q + 1, r, jnp.concatenate(halves, axis=1).astype(BF16).astype(F32))

    pool = Exchange(1, x_pool, halo_pool, edges_pool, recv_pool)
    skip = Exchange(2, x_skip, halo.at[1], edges.at[1], recv_skip)
    pool.send_rows()
    loads[2].wait()
    inner_rows(x_skip, acc_dec, dec_weights(1), 0, 1, False)
    pool.send_edges()
    skip.send_rows()
    inner_rows(x_skip, acc_dec, dec_weights(1), 1, inner, False)
    skip.send_edges()

    loads[3].wait()
    loads[4].wait()
    pool.wait_rows()

    acc_mid = acc_enc.at[0:hc, :, 0:cc, :]

    @pl.loop(0, hc // 2)
    def _(k):
        acc_enc[pl.ds(2 * k, 2), :, 0:cc, :] = conv_rows(x_pool, 2 * k, 2, mid_weights)

    pool.add_seams(acc_mid, lambda a, b: mid_w[a, b])

    @pl.loop(0, hc)
    def _(q):
        for r in range(cycles):
            value = gelu_tanh(acc_enc[q, r, 0:cc, :] + mid_b[...])
            coarse[q, r] = value.astype(BF16)

    @pl.loop(0, hc)
    def _(q):
        lhs = coarse[q].reshape(cycles * cc, ch)
        for a in range(2):
            for b in range(2):
                value = jnp.dot(lhs, up_w[a, b], preferred_element_type=F32) + up_b[...]
                for r in range(cycles):
                    for k in range(ch // 128):
                        fine[a, r, k, pl.ds(b, cc, stride=2), :] = value[
                            r * cc : (r + 1) * cc, k * 128 : (k + 1) * 128
                        ]
            for r in range(cycles):
                row = jnp.concatenate([fine[a, r, k] for k in range(ch // 128)], axis=1)
                spread(x_up, 2 * q + a + 1, r, row.astype(BF16).astype(F32))

    up = Exchange(3, x_up, halo.at[2], edges.at[2], recv_up)
    up.send_rows()
    skip.wait_rows()
    outer_rows(x_skip, acc_dec, dec_weights(1), False)
    up.send_edges()
    inner_rows(x_up, acc_dec, dec_weights(0), 0, inner, True)
    skip.add_seams(acc_dec, dec_tap(1))
    up.wait_rows()
    outer_rows(x_up, acc_dec, dec_weights(0), True)
    up.add_seams(acc_dec, dec_tap(0))

    @pl.loop(0, h)
    def _(i):
        for r in range(cycles):
            out[r, i] = (acc_dec[i, r] + dec_b[...]).astype(BF16)


def solution(mesh):
    tiles = mesh.shape["tile"]

    def on_device(fields, seam_tile, seam_code, enc_w, enc_b, mid_w, mid_b, up_w, up_b, dec_w, dec_b):
        cycles, h, cols, ch = fields.shape
        hc, cc = h // 2, cols // 2
        vmem = pl.BlockSpec(memory_space=pltpu.VMEM)
        smem = pl.BlockSpec(memory_space=pltpu.SMEM)
        hbm = pl.BlockSpec(memory_space=pl.ANY)
        ends = 2 * cycles
        slots = 2 * FACES
        return pl.pallas_call(
            functools.partial(kernel, tiles),
            out_shape=jax.ShapeDtypeStruct(fields.shape, BF16),
            in_specs=[smem, smem] + [hbm] * 5 + [vmem] * 4,
            out_specs=vmem,
            scratch_shapes=[
                pltpu.VMEM(fields.shape, BF16),
                pltpu.VMEM(enc_w.shape, BF16),
                pltpu.VMEM(mid_w.shape, BF16),
                pltpu.VMEM(up_w.shape, BF16),
                pltpu.VMEM(dec_w.shape, BF16),
                pltpu.VMEM((h + 2, cycles, cols, 3 * ch), BF16),
                pltpu.VMEM((h + 2, cycles, cols, 3 * ch), BF16),
                pltpu.VMEM((hc + 2, cycles, cc, 3 * ch), BF16),
                pltpu.VMEM((h + 2, cycles, cols, 3 * ch), BF16),
                pltpu.VMEM((h, cycles, cols, ch), F32),
                pltpu.VMEM((h, cycles, cols, ch), F32),
                pltpu.VMEM((hc, cycles, cc, ch), BF16),
                pltpu.VMEM((2, cycles, ch // 128, cols, 128), F32),
                pltpu.VMEM((cycles, ch // 128, cols, 128), F32),
                pltpu.VMEM((4, 2, 8, ch), F32),
                pltpu.VMEM((4, ends, 16, ch), F32),
                pltpu.VMEM((2, cycles, 16, ch), F32),
                pltpu.VMEM((4, 2, 8, ch), BF16),
                pltpu.VMEM((4, 2, 8, ch), BF16),
                pltpu.VMEM((3, 2, cycles, cols, ch), BF16),
                pltpu.VMEM((2, cycles, cc, ch), BF16),
                pltpu.VMEM((3, ends, h + 2, ch), BF16),
                pltpu.VMEM((ends, hc + 2, ch), BF16),
                pltpu.VMEM((slots, ends, h + 2, ch), BF16),
                pltpu.VMEM((slots, ends, h + 2, ch), BF16),
                pltpu.VMEM((slots, ends, h + 2, ch), BF16),
                pltpu.VMEM((slots, ends, hc + 2, ch), BF16),
                pltpu.SemaphoreType.DMA((5,)),
                pltpu.SemaphoreType.DMA((4, 4 + slots)),
                pltpu.SemaphoreType.DMA((4, 4 + slots)),
            ],
            compiler_params=pltpu.CompilerParams(
                collective_id=0, has_side_effects=True, vmem_limit_bytes=60 * 1024 * 1024
            ),
        )(
            seam_tile.reshape(cycles, 2),
            seam_code.reshape(cycles, 2),
            fields,
            enc_w,
            mid_w,
            up_w,
            dec_w,
            enc_b.reshape(1, ch),
            mid_b.reshape(1, ch),
            up_b.reshape(1, ch),
            dec_b.reshape(1, ch),
        )

    return jax.shard_map(
        on_device,
        mesh=mesh,
        in_specs=(P("grp", "tile", None, None), P(None, "tile", None), P(None, "tile", None)) + (P(),) * 8,
        out_specs=P("grp", "tile", None, None),
        check_vma=False,
    )
```

time: 165 us -> 61.3 us (0.37)
  blocking collectives: 65.8 us -> 0 us
  Pallas kernels: 0 us -> 55.8 us
  matrix products: 50.2 us -> 0 us
  local copies, waits for them, and re-layouts: 20.2 us -> 5.37 us
  other arithmetic: 12.4 us -> 0 us
  starting transfers between devices: 11.5 us -> 0 us
  waiting for transfers between devices: 3.92 us -> 0 us
    all_gather x3 -> x0, blocking collectives: 65.8 us -> none  [the longest x2 40.8 us: on_device(): lax.all_gather(boundary_columns(extended)[:, None], 'tile', axis=1, tiled...]
    pallas_call x0 -> x1, Pallas kernels: none -> 55.8 us  [on_device(): pl.pallas_call(functools.partial(kernel, tiles), out_shape=jax.ShapeDtype...]
    dot_general x31 -> x0, matrix products: 50.2 us -> none  [the longest x27 49.1 us: convolve(): jnp.dot(window.reshape(-1, chans_in), weight[row_tap, col_tap], preferred...]
    ppermute x6 -> x0, starting transfers between devices: 11.5 us -> none  [the longest x3 10.5 us: with_halo(): after = lax.ppermute(first, axis, down)]
    concatenate x3 -> x0, other arithmetic: 4.9 us -> none  [attach_columns(): return jnp.concatenate([left_col, extended, right_col], axis=-2)]
    reduce_sum x1 -> x0, other arithmetic: 4.28 us -> none  [coarsen_grid(): return jnp.mean(values, axis=(-4, -2)).astype(jnp.bfloat16)]
    gather x3 -> x0, local copies, waits for them, and re-layouts: 4.01 us -> none  [pick_partner(): chosen = flattened[partners]]
    ppermute x6 -> x0, waiting for transfers between devices: 3.92 us -> none  [the longest x3 2.24 us: with_halo(): before = lax.ppermute(last, axis, up)]
  transfers between devices with their start and end apart: 6 -> 0, of which waited for: 3 -> 0; matrix products, arithmetic and copies ran while one was open for 10% -> 0% of each run, Pallas kernels for 0% -> 0%
where the time goes in v1:
time: 61.3 us; the launch traced here: 61.1 us
  Pallas kernels  55.8 us (91%)
  local copies, waits for them, and re-layouts  5.37 us (9%)
    pallas_call x1, Pallas kernels, on_device(): pl.pallas_call(functools.partial(kernel, tiles), out_shape=jax.ShapeDtype...  55.8 us
    unnamed x1, local copies, waits for them, and re-layouts  2.7 us
    reshape x1, local copies, waits for them, and re-layouts, on_device(): seam_tile.reshape(cycles, 2)  1.34 us
    reshape x1, local copies, waits for them, and re-layouts, on_device(): seam_code.reshape(cycles, 2)  1.33 us

profile of v1, /device:TPU:0, one launch (start us, length us, event | category | flops | bytes accessed | tf_op | source)
XLA Modules:
  0.0 61.1 jit_solution(2774377767948728943)
XLA Ops:
  0.0 1.3 %copy.12.seam_tile = s32[3,2]{1,0:T(4,128)} copy(s32[3,2]{0,1:T(2,128)} %bitcast.10) | data formatting | bytes 48 | tf_op jit(solution)/shard_map/reshape | solution.py:414
  1.3 1.3 %copy.13.seam_code = s32[3,2]{1,0:T(4,128)} copy(s32[3,2]{0,1:T(2,128)} %bitcast.11) | data formatting | bytes 48 | tf_op jit(solution)/shard_map/reshape | solution.py:415
  2.7 55.8 %shard_map.109 = bf16[3,8,128,256]{3,2,1,0:T(8,128)(2,1)} custom-call(s32[3,2]{1,0:T(4,128)} %copy.12.seam_tile, s32[3,2]{1,0:T(4,128)} %copy.13.seam_code, bf16[3,8,128,256]{3,2,1,0:T(8,128)(2,1)} %fields_hbm.1, bf16[3,3,256,256]{3,2,1,0:T(8,128)(2,1)} %enc_w_hbm.1, bf16[3,3,256,256]{3,2,1,0:T(8,128)(2,1)} %mid_w_hbm.1, bf16[2,2,256,256]{3,2,1,0:T(8,128)(2,1)} %up_w_hbm.1, ...), custom_call_target="tpu_custom_call" | custom-call | tf_op jit(solution)/shard_map/pallas_call | solution.py:373
  58.4 2.7 %copy.15 = bf16[3,8,128,256]{3,2,1,0:T(8,128)(2,1)} copy(bf16[3,8,128,256]{3,2,1,0:T(8,128)(2,1)} %shard_map.109) | data formatting | bytes 3145728

commit v2 on v1

--- a/solution.py
+++ b/solution.py
@@ -49,6 +49,7 @@
     seam_tmp,
     corner_src,
     corner_dst,
+    corners,
     halo,
     halo_pool,
     edges,
@@ -57,10 +58,15 @@
     recv_skip,
     recv_up,
     recv_pool,
+    corner_enc,
+    corner_pool,
+    corner_skip,
+    corner_up,
     load_sem,
     send_sem,
     recv_sem,
 ):
+    recv_corners = (corner_enc, corner_pool, corner_skip, corner_up)
     cycles, h, cols, ch = fields.shape
     hc, cc = h // 2, cols // 2
     strips = tiles // FACES
@@ -95,7 +101,6 @@
     targets = [up_tile, down_tile] + [peer for _, _, peer in peers]
     for target in targets:
         pl.semaphore_signal(barrier, inc=1, device_id={"tile": target})
-    pl.semaphore_wait(barrier, len(targets))
 
     def remote(src, dst, e, send_at, recv_at, target):
         return pltpu.make_async_remote_copy(
@@ -116,50 +121,48 @@
         x[i, r, :, 2 * ch : 3 * ch] = right.astype(BF16)
 
     class Exchange:
-        def __init__(self, e, x, halo_ref, edge_ref, recv_ref):
+        def __init__(self, e, x, halo_ref, edge_ref, recv_ref, source=None):
             self.e, self.x, self.halo, self.edges, self.recv = e, x, halo_ref, edge_ref, recv_ref
             self.rows = x.shape[0] - 2
             self.width = x.shape[2]
+            self.source = source
+
+        def row(self, i):
+            if self.source is None:
+                return self.x.at[i + 1, :, :, ch : 2 * ch]
+            return self.source.at[:, i]
 
         def end_pixels(self, i, r):
-            head = self.x[i, r, 0:16, ch : 2 * ch].astype(F32)[0:1]
-            tail = self.x[i, r, self.width - 16 : self.width, ch : 2 * ch].astype(F32)[15:16]
+            row = self.row(i)
+            head = row[r, 0:16, :].astype(F32)[0:1]
+            tail = row[r, self.width - 16 : self.width, :].astype(F32)[15:16]
             return head, tail
 
-        def send_rows(self):
-            e, x, rows = self.e, self.x, self.rows
-            for which, i in ((0, 1), (1, rows)):
-                for r in range(cycles):
-                    head, tail = self.end_pixels(i, r)
-                    corner_tmp[e, which, 2 * r : 2 * r + 1, :] = head
-                    corner_tmp[e, which, 2 * r + 1 : 2 * r + 2, :] = tail
+        def prepare(self):
+            e, rows = self.e, self.rows
+            for r in range(cycles):
+                for i in range(rows):
+                    for side, pixel in enumerate(self.end_pixels(i, r)):
+                        k = 2 * r + side
+                        edge_tmp[e, k, i : i + 1, :] = pixel
+                        if i == 0:
+                            corner_tmp[e, 0, k : k + 1, :] = pixel
+                        if i == rows - 1:
+                            corner_tmp[e, 1, k : k + 1, :] = pixel
+            for which in range(2):
                 corner_src[e, which] = corner_tmp[e, which].astype(BF16)
+            value = edge_tmp[e, :, 0:rows, :].astype(BF16)
+            self.edges[...] = value
+            self.recv[face] = value
+
+        def send(self):
+            e, rows = self.e, self.rows
             self.copies = [
                 remote(corner_src.at[e, 1], corner_dst.at[e, 0], e, 0, 0, down_tile),
                 remote(corner_src.at[e, 0], corner_dst.at[e, 1], e, 1, 1, up_tile),
-                remote(x.at[rows, :, :, ch : 2 * ch], self.halo.at[0], e, 2, 2, down_tile),
-                remote(x.at[1, :, :, ch : 2 * ch], self.halo.at[1], e, 3, 3, up_tile),
+                remote(self.row(rows - 1), self.halo.at[0], e, 2, 2, down_tile),
+                remote(self.row(0), self.halo.at[1], e, 3, 3, up_tile),
             ]
-            for copy in self.copies:
-                copy.start()
-
-        def send_edges(self):
-            e, rows = self.e, self.rows
-            self.copies[0].wait_recv()
-            self.copies[1].wait_recv()
-            above = jnp.where(top_face, 0.0, corner_dst[e, 0].astype(F32))
-            below = jnp.where(bottom_face, 0.0, corner_dst[e, 1].astype(F32))
-            for r in range(cycles):
-                for side in range(2):
-                    k = 2 * r + side
-                    edge_tmp[e, k, 0:1, :] = above[k : k + 1]
-                    edge_tmp[e, k, rows + 1 : rows + 2, :] = below[k : k + 1]
-                for i in range(rows):
-                    for side, pixel in enumerate(self.end_pixels(i + 1, r)):
-                        edge_tmp[e, 2 * r + side, i + 1 : i + 2, :] = pixel
-            value = edge_tmp[e, :, 0 : rows + 2, :].astype(BF16)
-            self.edges[...] = value
-            self.recv[face] = value
             self.seams = [
                 remote(
                     self.edges,
@@ -171,7 +174,31 @@
                 )
                 for kind, f, peer in peers
             ]
-            for copy in self.seams:
+            for copy in self.copies[0:2] + self.seams + self.copies[2:4]:
+                copy.start()
+
+        def relay(self):
+            e = self.e
+            self.copies[0].wait_recv()
+            self.copies[1].wait_recv()
+            above = jnp.where(top_face, 0.0, corner_dst[e, 0].astype(F32))
+            below = jnp.where(bottom_face, 0.0, corner_dst[e, 1].astype(F32))
+            value = jnp.concatenate([above, below], axis=0).astype(BF16)
+            corners[e] = value
+            self.recv_corner = recv_corners[e]
+            self.recv_corner[face] = value
+            self.relays = [
+                remote(
+                    corners.at[e],
+                    self.recv_corner.at[kind * FACES + face],
+                    e,
+                    12 + kind * FACES + f,
+                    12 + kind * FACES + face,
+                    peer,
+                )
+                for kind, f, peer in peers
+            ]
+            for copy in self.relays:
                 copy.start()
 
         def wait_rows(self):
@@ -183,14 +210,20 @@
                 below = jnp.where(bottom_face, 0.0, self.halo[1, r].astype(F32))
                 spread(self.x, self.rows + 1, r, below)
 
-        def seam_terms(self, weight_of):
-            e, rows = self.e, self.rows
+        def wait_seams(self):
+            e = self.e
             for kind, f, peer in peers:
                 slot = kind * FACES + f
                 remote(self.edges, self.recv.at[slot], e, 4 + slot, 4 + slot, peer).wait_recv()
-            for copy in self.copies + self.seams:
+                remote(
+                    corners.at[e], self.recv_corner.at[slot], e, 12 + slot, 12 + slot, peer
+                ).wait_recv()
+            for copy in self.copies + self.seams + self.relays:
                 copy.wait_send()
-            terms = []
+
+        def load_seams(self):
+            rows = self.rows
+            at = lax.broadcasted_iota(jnp.int32, (8, ch), 0)
             for side in range(2):
                 for r in range(cycles):
                     partner, code = seam_tile[r, side], seam_code[r, side]
@@ -198,28 +231,30 @@
                     home = lax.rem(partner - cycle * tiles + strips // 2, tiles) // strips
                     mirrored = code >= 2
                     slot = jnp.where(mirrored, FACES, 0) + home
-                    column = self.recv[slot, 2 * cycle + lax.rem(code, 2)].astype(F32)
-                    for i in range(rows + 2):
-                        seam_tmp[side, r, i : i + 1, :] = jnp.where(
-                            mirrored, column[rows + 1 - i : rows + 2 - i], column[i : i + 1]
+                    k = 2 * cycle + lax.rem(code, 2)
+                    column = self.recv[slot, k].astype(F32)
+                    ends = self.recv_corner[slot].astype(F32)
+                    above = jnp.sum(jnp.where(at == k, ends[0:8], 0.0), axis=0, keepdims=True)
+                    below = jnp.sum(jnp.where(at == k, ends[8:16], 0.0), axis=0, keepdims=True)
+                    seam_tmp[side, r, 0:1, :] = jnp.where(mirrored, below, above)
+                    seam_tmp[side, r, rows + 1 : rows + 2, :] = jnp.where(mirrored, above, below)
+                    for i in range(rows):
+                        seam_tmp[side, r, i + 1 : i + 2, :] = jnp.where(
+                            mirrored, column[rows - 1 - i : rows - i], column[i : i + 1]
                         )
-                taps = [
-                    jnp.concatenate([seam_tmp[side, r, a : a + 8, :] for r in range(cycles)], axis=0).astype(BF16)
-                    for a in range(3)
-                ]
+
+        def add_seams(self, acc, weight_of):
+            self.wait_seams()
+            self.load_seams()
+            for side in range(2):
+                j = 0 if side == 0 else self.width - 1
                 term = jnp.zeros((8 * cycles, ch), F32)
                 for a in range(3):
-                    term = term + jnp.dot(taps[a], weight_of(a, 2 * side), preferred_element_type=F32)
-                terms.append(term)
-            return terms
-
-        def add_seams(self, acc, weight_of):
-            terms = self.seam_terms(weight_of)
-            for side in range(2):
-                j = 0 if side == 0 else self.width - 1
+                    tap = jnp.concatenate([seam_tmp[side, r, a : a + 8, :] for r in range(cycles)], axis=0)
+                    term = term + jnp.dot(tap.astype(BF16), weight_of(a, 2 * side), preferred_element_type=F32)
                 for r in range(cycles):
                     for i in range(self.rows):
-                        acc[i, r, j : j + 1, :] += terms[side][8 * r + i : 8 * r + i + 1]
+                        acc[i, r, j : j + 1, :] += term[8 * r + i : 8 * r + i + 1]
 
     def conv_rows(x, start, count, weights):
         width = x.shape[2]
@@ -244,14 +279,16 @@
         return lambda a, b: dec_w[a, b, part * ch : (part + 1) * ch, :]
 
     loads[0].wait()
+    enc = Exchange(0, x_enc, halo.at[0], edges.at[0], recv_enc, fields)
+    enc.prepare()
+    pl.semaphore_wait(barrier, len(targets))
+    enc.send()
 
     @pl.loop(0, h)
     def _(i):
         for r in range(cycles):
             spread(x_enc, i + 1, r, fields[r, i].astype(F32))
 
-    enc = Exchange(0, x_enc, halo.at[0], edges.at[0], recv_enc)
-    enc.send_rows()
     loads[1].wait()
 
     def inner_rows(x, acc, weights, lo, hi, add):
@@ -265,9 +302,8 @@
                 acc[pl.ds(start, 2)] = value
 
     inner = (h - 2) // 2
-    inner_rows(x_enc, acc_enc, enc_weights, 0, 1, False)
-    enc.send_edges()
-    inner_rows(x_enc, acc_enc, enc_weights, 1, inner, False)
+    enc.relay()
+    inner_rows(x_enc, acc_enc, enc_weights, 0, inner, False)
     enc.wait_rows()
 
     def outer_rows(x, acc, weights, add):
@@ -301,13 +337,14 @@
 
     pool = Exchange(1, x_pool, halo_pool, edges_pool, recv_pool)
     skip = Exchange(2, x_skip, halo.at[1], edges.at[1], recv_skip)
-    pool.send_rows()
+    pool.prepare()
+    pool.send()
+    skip.prepare()
     loads[2].wait()
     inner_rows(x_skip, acc_dec, dec_weights(1), 0, 1, False)
-    pool.send_edges()
-    skip.send_rows()
+    pool.relay()
     inner_rows(x_skip, acc_dec, dec_weights(1), 1, inner, False)
-    skip.send_edges()
+    skip.send()
 
     loads[3].wait()
     loads[4].wait()
@@ -343,10 +380,12 @@
                 spread(x_up, 2 * q + a + 1, r, row.astype(BF16).astype(F32))
 
     up = Exchange(3, x_up, halo.at[2], edges.at[2], recv_up)
-    up.send_rows()
+    up.prepare()
+    up.send()
+    skip.relay()
     skip.wait_rows()
     outer_rows(x_skip, acc_dec, dec_weights(1), False)
-    up.send_edges()
+    up.relay()
     inner_rows(x_up, acc_dec, dec_weights(0), 0, inner, True)
     skip.add_seams(acc_dec, dec_tap(1))
     up.wait_rows()
@@ -391,21 +430,26 @@
                 pltpu.VMEM((2, cycles, ch // 128, cols, 128), F32),
                 pltpu.VMEM((cycles, ch // 128, cols, 128), F32),
                 pltpu.VMEM((4, 2, 8, ch), F32),
-                pltpu.VMEM((4, ends, 16, ch), F32),
+                pltpu.VMEM((4, ends, 8, ch), F32),
                 pltpu.VMEM((2, cycles, 16, ch), F32),
                 pltpu.VMEM((4, 2, 8, ch), BF16),
                 pltpu.VMEM((4, 2, 8, ch), BF16),
+                pltpu.VMEM((4, 16, ch), BF16),
                 pltpu.VMEM((3, 2, cycles, cols, ch), BF16),
                 pltpu.VMEM((2, cycles, cc, ch), BF16),
-                pltpu.VMEM((3, ends, h + 2, ch), BF16),
-                pltpu.VMEM((ends, hc + 2, ch), BF16),
-                pltpu.VMEM((slots, ends, h + 2, ch), BF16),
-                pltpu.VMEM((slots, ends, h + 2, ch), BF16),
-                pltpu.VMEM((slots, ends, h + 2, ch), BF16),
-                pltpu.VMEM((slots, ends, hc + 2, ch), BF16),
+                pltpu.VMEM((3, ends, h, ch), BF16),
+                pltpu.VMEM((ends, hc, ch), BF16),
+                pltpu.VMEM((slots, ends, h, ch), BF16),
+                pltpu.VMEM((slots, ends, h, ch), BF16),
+                pltpu.VMEM((slots, ends, h, ch), BF16),
+                pltpu.VMEM((slots, ends, hc, ch), BF16),
+                pltpu.VMEM((slots, 16, ch), BF16),
+                pltpu.VMEM((slots, 16, ch), BF16),
+                pltpu.VMEM((slots, 16, ch), BF16),
+                pltpu.VMEM((slots, 16, ch), BF16),
                 pltpu.SemaphoreType.DMA((5,)),
-                pltpu.SemaphoreType.DMA((4, 4 + slots)),
-                pltpu.SemaphoreType.DMA((4, 4 + slots)),
+                pltpu.SemaphoreType.DMA((4, 4 + 2 * slots)),
+                pltpu.SemaphoreType.DMA((4, 4 + 2 * slots)),
             ],
             compiler_params=pltpu.CompilerParams(
                 collective_id=0, has_side_effects=True, vmem_limit_bytes=60 * 1024 * 1024

time: 61.3 us -> 52.7 us (0.86)
  Pallas kernels: 55.8 us -> 47.1 us
    pallas_call x1, Pallas kernels: 55.8 us -> 47.1 us  [on_device(): pl.pallas_call(functools.partial(kernel, tiles), out_shape=jax.ShapeDtype...]
where the time goes in v2:
time: 52.7 us; the launch traced here: 52.5 us
  Pallas kernels  47.1 us (89%)
  local copies, waits for them, and re-layouts  5.37 us (10%)
    pallas_call x1, Pallas kernels, on_device(): pl.pallas_call(functools.partial(kernel, tiles), out_shape=jax.ShapeDtype...  47.1 us
    unnamed x1, local copies, waits for them, and re-layouts  2.7 us
    reshape x1, local copies, waits for them, and re-layouts, on_device(): seam_tile.reshape(cycles, 2)  1.34 us
    reshape x1, local copies, waits for them, and re-layouts, on_device(): seam_code.reshape(cycles, 2)  1.33 us

profile of v2, /device:TPU:0, one launch (start us, length us, event | category | flops | bytes accessed | tf_op | source)
XLA Modules:
  0.0 52.5 jit_solution(13844601083627357387)
XLA Ops:
  0.0 1.3 %copy.12.seam_tile = s32[3,2]{1,0:T(4,128)} copy(s32[3,2]{0,1:T(2,128)} %bitcast.10) | data formatting | bytes 48 | tf_op jit(solution)/shard_map/reshape | solution.py:458
  1.3 1.3 %copy.13.seam_code = s32[3,2]{1,0:T(4,128)} copy(s32[3,2]{0,1:T(2,128)} %bitcast.11) | data formatting | bytes 48 | tf_op jit(solution)/shard_map/reshape | solution.py:459
  2.7 47.1 %shard_map.109 = bf16[3,8,128,256]{3,2,1,0:T(8,128)(2,1)} custom-call(s32[3,2]{1,0:T(4,128)} %copy.12.seam_tile, s32[3,2]{1,0:T(4,128)} %copy.13.seam_code, bf16[3,8,128,256]{3,2,1,0:T(8,128)(2,1)} %fields_hbm.1, bf16[3,3,256,256]{3,2,1,0:T(8,128)(2,1)} %enc_w_hbm.1, bf16[3,3,256,256]{3,2,1,0:T(8,128)(2,1)} %mid_w_hbm.1, bf16[2,2,256,256]{3,2,1,0:T(8,128)(2,1)} %up_w_hbm.1, ...), custom_call_target="tpu_custom_call" | custom-call | tf_op jit(solution)/shard_map/pallas_call | solution.py:412
  49.8 2.7 %copy.15 = bf16[3,8,128,256]{3,2,1,0:T(8,128)(2,1)} copy(bf16[3,8,128,256]{3,2,1,0:T(8,128)(2,1)} %shard_map.109) | data formatting | bytes 3145728

commit v3 on v2

--- a/solution.py
+++ b/solution.py
@@ -281,13 +281,13 @@
     loads[0].wait()
     enc = Exchange(0, x_enc, halo.at[0], edges.at[0], recv_enc, fields)
     enc.prepare()
-    pl.semaphore_wait(barrier, len(targets))
-    enc.send()
-
     @pl.loop(0, h)
     def _(i):
         for r in range(cycles):
             spread(x_enc, i + 1, r, fields[r, i].astype(F32))
+
+    pl.semaphore_wait(barrier, len(targets))
+    enc.send()
 
     loads[1].wait()
 
@@ -302,9 +302,6 @@
                 acc[pl.ds(start, 2)] = value
 
     inner = (h - 2) // 2
-    enc.relay()
-    inner_rows(x_enc, acc_enc, enc_weights, 0, inner, False)
-    enc.wait_rows()
 
     def outer_rows(x, acc, weights, add):
         @pl.loop(0, 2)
@@ -316,6 +313,10 @@
             else:
                 acc[pl.ds(i, 1)] = value
 
+    inner_rows(x_enc, acc_enc, enc_weights, 0, 1, False)
+    enc.relay()
+    inner_rows(x_enc, acc_enc, enc_weights, 1, inner, False)
+    enc.wait_rows()
     outer_rows(x_enc, acc_enc, enc_weights, False)
     enc.add_seams(acc_enc, lambda a, b: enc_w[a, b])
 
@@ -356,6 +357,7 @@
     def _(k):
         acc_enc[pl.ds(2 * k, 2), :, 0:cc, :] = conv_rows(x_pool, 2 * k, 2, mid_weights)
 
+    skip.relay()
     pool.add_seams(acc_mid, lambda a, b: mid_w[a, b])
 
     @pl.loop(0, hc)
@@ -382,7 +384,6 @@
     up = Exchange(3, x_up, halo.at[2], edges.at[2], recv_up)
     up.prepare()
     up.send()
-    skip.relay()
     skip.wait_rows()
     outer_rows(x_skip, acc_dec, dec_weights(1), False)
     up.relay()

time: 52.7 us -> 51.5 us (0.977)
  Pallas kernels: 47.1 us -> 45.9 us
    pallas_call x1, Pallas kernels: 47.1 us -> 45.9 us  [on_device(): pl.pallas_call(functools.partial(kernel, tiles), out_shape=jax.ShapeDtype...]
where the time goes in v3:
time: 51.5 us; the launch traced here: 51.3 us
  Pallas kernels  45.9 us (89%)
  local copies, waits for them, and re-layouts  5.37 us (10%)
    pallas_call x1, Pallas kernels, on_device(): pl.pallas_call(functools.partial(kernel, tiles), out_shape=jax.ShapeDtype...  45.9 us
    unnamed x1, local copies, waits for them, and re-layouts  2.7 us
    reshape x1, local copies, waits for them, and re-layouts, on_device(): seam_tile.reshape(cycles, 2)  1.34 us
    reshape x1, local copies, waits for them, and re-layouts, on_device(): seam_code.reshape(cycles, 2)  1.33 us

profile of v3, /device:TPU:0, one launch (start us, length us, event | category | flops | bytes accessed | tf_op | source)
XLA Modules:
  0.0 51.3 jit_solution(2241918187934877575)
XLA Ops:
  0.0 1.3 %copy.12.seam_tile = s32[3,2]{1,0:T(4,128)} copy(s32[3,2]{0,1:T(2,128)} %bitcast.10) | data formatting | bytes 48 | tf_op jit(solution)/shard_map/reshape | solution.py:459
  1.3 1.3 %copy.13.seam_code = s32[3,2]{1,0:T(4,128)} copy(s32[3,2]{0,1:T(2,128)} %bitcast.11) | data formatting | bytes 48 | tf_op jit(solution)/shard_map/reshape | solution.py:460
  2.7 45.9 %shard_map.109 = bf16[3,8,128,256]{3,2,1,0:T(8,128)(2,1)} custom-call(s32[3,2]{1,0:T(4,128)} %copy.12.seam_tile, s32[3,2]{1,0:T(4,128)} %copy.13.seam_code, bf16[3,8,128,256]{3,2,1,0:T(8,128)(2,1)} %fields_hbm.1, bf16[3,3,256,256]{3,2,1,0:T(8,128)(2,1)} %enc_w_hbm.1, bf16[3,3,256,256]{3,2,1,0:T(8,128)(2,1)} %mid_w_hbm.1, bf16[2,2,256,256]{3,2,1,0:T(8,128)(2,1)} %up_w_hbm.1, ...), custom_call_target="tpu_custom_call" | custom-call | tf_op jit(solution)/shard_map/pallas_call | solution.py:413
  48.6 2.7 %copy.15 = bf16[3,8,128,256]{3,2,1,0:T(8,128)(2,1)} copy(bf16[3,8,128,256]{3,2,1,0:T(8,128)(2,1)} %shard_map.109) | data formatting | bytes 3145728

commit v4 on v3

--- a/solution.py
+++ b/solution.py
@@ -344,8 +344,8 @@
     loads[2].wait()
     inner_rows(x_skip, acc_dec, dec_weights(1), 0, 1, False)
     pool.relay()
+    skip.send()
     inner_rows(x_skip, acc_dec, dec_weights(1), 1, inner, False)
-    skip.send()
 
     loads[3].wait()
     loads[4].wait()

time: 51.5 us -> 51.4 us (level)
  no operation moved by 1% of the time
where the time goes in v4:
time: 51.4 us; the launch traced here: 51.2 us
  Pallas kernels  45.8 us (89%)
  local copies, waits for them, and re-layouts  5.37 us (10%)
    pallas_call x1, Pallas kernels, on_device(): pl.pallas_call(functools.partial(kernel, tiles), out_shape=jax.ShapeDtype...  45.8 us
    unnamed x1, local copies, waits for them, and re-layouts  2.7 us
    reshape x1, local copies, waits for them, and re-layouts, on_device(): seam_tile.reshape(cycles, 2)  1.34 us
    reshape x1, local copies, waits for them, and re-layouts, on_device(): seam_code.reshape(cycles, 2)  1.33 us

profile of v4, /device:TPU:0, one launch (start us, length us, event | category | flops | bytes accessed | tf_op | source)
XLA Modules:
  0.0 51.2 jit_solution(13351546167521907058)
XLA Ops:
  0.0 1.3 %copy.12.seam_tile = s32[3,2]{1,0:T(4,128)} copy(s32[3,2]{0,1:T(2,128)} %bitcast.10) | data formatting | bytes 48 | tf_op jit(solution)/shard_map/reshape | solution.py:459
  1.3 1.3 %copy.13.seam_code = s32[3,2]{1,0:T(4,128)} copy(s32[3,2]{0,1:T(2,128)} %bitcast.11) | data formatting | bytes 48 | tf_op jit(solution)/shard_map/reshape | solution.py:460
  2.7 45.8 %shard_map.109 = bf16[3,8,128,256]{3,2,1,0:T(8,128)(2,1)} custom-call(s32[3,2]{1,0:T(4,128)} %copy.12.seam_tile, s32[3,2]{1,0:T(4,128)} %copy.13.seam_code, bf16[3,8,128,256]{3,2,1,0:T(8,128)(2,1)} %fields_hbm.1, bf16[3,3,256,256]{3,2,1,0:T(8,128)(2,1)} %enc_w_hbm.1, bf16[3,3,256,256]{3,2,1,0:T(8,128)(2,1)} %mid_w_hbm.1, bf16[2,2,256,256]{3,2,1,0:T(8,128)(2,1)} %up_w_hbm.1, ...), custom_call_target="tpu_custom_call" | custom-call | tf_op jit(solution)/shard_map/pallas_call | solution.py:413
  48.5 2.7 %copy.15 = bf16[3,8,128,256]{3,2,1,0:T(8,128)(2,1)} copy(bf16[3,8,128,256]{3,2,1,0:T(8,128)(2,1)} %shard_map.109) | data formatting | bytes 3145728
